TPU v7x, 128 devices: a whole 4x4x4 slice. The times are simulated.
128 devices in a mesh: patch: 16 (over y, x), col: 8 (over z, core).
Axes of the slice: x: 4, y: 4, z: 4, core: 2. Of those that a mesh axis runs over, the one named last changes fastest.
Arguments:
- potential0: float32 [512, 16, 128], P(('patch', 'col')), may hold values from -3 to 3
- source_term: float32 [512, 16, 128], P(('patch', 'col')), may hold values from -9 to 9
- self_coef: float32 [512, 128], P(('patch', 'col')), may hold values from 1 to 4
- nearfield: float32 [512, 24, 128, 128], P(('patch', 'col')), may hold values from -0.109375 to 0.109375
- precond: float32 [512, 128, 128], P(('patch', 'col')), may hold values from -1 to 2
- exch_current: float32 [512, 128], P(('patch', 'col')), may hold values from 0.05 to 0.5
- conductance: float32 [512, 128], P(('patch', 'col')), may hold values from 0.1 to 1
- member: int32 [512, 128], P(('patch', 'col')), may hold values from 0 to 63
- anode_drive: float32 [64], replicated, may hold values from -1 to 1
- pair_source: int32 [512, 24], P(('patch', 'col')), may hold values from 0 to 39
- pair_count: int32 [512], P(('patch', 'col')), may hold values from 1 to 24, as said below
Outputs:
- potential: float32 [512, 16, 128], P(('patch', 'col'))
- residual: float32 [512, 16, 128], P(('patch', 'col'))
Inputs may be any that keep to these rules, and one draw needn't show every extreme that they name: Slots k < pair_count[b] of block b are live; some block has all 24 slots live, and the blocks of some devices hold far more live pairs than those of others.
All inputs are finite; a program needn't handle non-finite values.
Results may differ from a plain program's by a relative error of at most 0.0003.
Values sent between devices are 32-bit elements; how exact they have to be, the bound alone decides.
A program may use at most 64 MiB of HBM per device.

v0:
```python
import jax
import jax.numpy as jnp
from jax import lax
from jax.sharding import PartitionSpec as P

NEWTON = 2
GMRES = 2
ALPHA = 0.6
BETA = 0.4
EPS = 1e-06


def from_behind(array, axis, by):
    size = lax.axis_size(axis)
    return lax.ppermute(array, axis, [(i, (i + by) % size) for i in range(size)])


def column_sum(left, right):
    return jnp.sum(left * right, axis=(0, 2))


def least_squares(columns, beta):
    depth = len(columns)
    hessen = jnp.zeros((beta.shape[0], depth + 1, depth), jnp.float32)
    for place in range(depth):
        hessen = hessen.at[:, : place + 2, place].set(columns[place].T)
    gram = jnp.einsum("cij,cik->cjk", hessen, hessen, precision=lax.Precision.HIGHEST)
    right = beta[:, None] * hessen[:, 0, :]
    lower = jnp.linalg.cholesky(gram)
    middle = jax.scipy.linalg.solve_triangular(lower, right[:, :, None], lower=True)
    return jax.scipy.linalg.solve_triangular(lower, middle, lower=True, trans=1)[:, :, 0]


def body(
    potential0,
    source_term,
    self_coef,
    nearfield,
    precond,
    exch_current,
    conductance,
    member,
    anode_drive,
    pair_source,
    pair_count,
):
    pair_slots = pair_source.shape[1]
    live_mask = (jnp.arange(pair_slots, dtype=jnp.int32)[None, :] < pair_count[:, None]).astype(
        jnp.float32
    )
    members = anode_drive.shape[0]
    onehot = (jnp.arange(members, dtype=jnp.int32)[:, None, None] == member[None]).astype(
        jnp.float32
    )
    member_drive = jnp.sum(onehot * anode_drive[:, None, None], axis=0)
    diagonal = self_coef[:, None, :]
    current = exch_current[:, None, :]
    conduct = conductance[:, None, :]

    def near_field(field):
        own_patch = lax.all_gather(field, "col", axis=0, tiled=True)
        before = from_behind(field, "patch", 1)
        following = from_behind(field, "patch", -1)
        stacked = jnp.concatenate([own_patch, before, following], axis=0)
        sources = stacked[pair_source]
        return jnp.einsum(
            "bkij,bkcj->bci",
            nearfield,
            sources * live_mask[:, :, None, None],
            precision=lax.Precision.HIGHEST,
        )

    def mismatch(field, near_value):
        grow = jnp.exp(ALPHA * field)
        shrink = jnp.exp(-BETA * field)
        value = (
            diagonal * field
            + near_value
            + current * (grow - shrink)
            + conduct * (field - member_drive[:, None, :])
            - source_term
        )
        slope = current * (ALPHA * grow + BETA * shrink) + conduct
        return (value, slope)

    field = potential0
    near_now = near_field(field)
    for newton in range(NEWTON):
        value, slope = mismatch(field, near_now)
        start = -value
        beta = jnp.sqrt(lax.psum(column_sum(start, start), ("patch", "col")) + EPS)
        basis = [start / beta[None, :, None]]
        directions = []
        near_images = []
        columns = []
        for step in range(GMRES):
            direction = jnp.einsum(
                "bij,bcj->bci", precond, basis[step], precision=lax.Precision.HIGHEST
            )
            directions.append(direction)
            near_image = near_field(direction)
            near_images.append(near_image)
            image = diagonal * direction + near_image + slope * direction
            coeffs = []
            for place in range(step + 1):
                coeff = lax.psum(column_sum(basis[place], image), ("patch", "col"))
                image = image - coeff[None, :, None] * basis[place]
                coeffs.append(coeff)
            norm = jnp.sqrt(lax.psum(column_sum(image, image), ("patch", "col")) + EPS)
            basis.append(image / norm[None, :, None])
            columns.append(jnp.stack(coeffs + [norm]))
        weights = least_squares(columns, beta)
        update = jnp.zeros_like(field)
        for step in range(GMRES):
            update = update + weights[:, step][None, :, None] * directions[step]
        field = field + update
        near_now = near_field(field)
    final_value, final_slope = mismatch(field, near_now)
    return (field, final_value)


def solution(mesh):
    return jax.shard_map(
        body,
        mesh=mesh,
        in_specs=(
            P(("patch", "col"), None, None),
            P(("patch", "col"), None, None),
            P(("patch", "col"), None),
            P(("patch", "col"), None, None, None),
            P(("patch", "col"), None, None),
            P(("patch", "col"), None),
            P(("patch", "col"), None),
            P(("patch", "col"), None),
            P(),
            P(("patch", "col"), None),
            P(("patch", "col")),
        ),
        out_specs=(P(("patch", "col"), None, None), P(("patch", "col"), None, None)),
        check_vma=False,
    )
```

profile of v0, /device:TPU:1, one launch (start us, length us, event | category | flops | bytes accessed | tf_op | source)
XLA Modules:
  0.0 974.0 jit_solution(4111155873102971596)
XLA Ops:
  2.8 3.8 collective-permute-start.1
  6.6 15.1 %all_gather.21 = f32[32,16,128]{2,1,0:T(8,128)S(1)} all-gather(f32[4,16,128]{2,1,0:T(8,128)} %param.24), channel_id=1, replica_groups=mesh['patch'=16,'col'=8] {'col'}, dimensions={0}, use_global_device_ids=true | all-gather | bytes 294912 | tf_op jit(solution)/shard_map/all_gather | solution.py:61
  24.7 7.6 multiply_reduce_fusion.11
  32.3 64.2 %psum.84 = f32[16]{0:T(128)S(1)} all-reduce(f32[16]{0:T(128)S(1)} %get-tuple-element.61), channel_id=1, replica_groups=mesh['patch'=16,'col'=8] {'patch','col'}, use_global_device_ids=true, to_apply=%region_2.0 | all-reduce | flops 16 | bytes 128 | tf_op jit(solution)/shard_map/psum | solution.py:91
  97.3 4.6 collective-permute-start.3
  101.9 13.9 %all_gather.22 = f32[32,16,128]{2,1,0:T(8,128)S(1)} all-gather(f32[4,16,128]{2,1,0:T(8,128)S(1)} %fusion.43), channel_id=1, replica_groups=mesh['patch'=16,'col'=8] {'col'}, dimensions={0}, use_global_device_ids=true | all-gather | bytes 294912 | tf_op jit(solution)/shard_map/all_gather | solution.py:61
  116.5 7.5 multiply_reduce_fusion.10
  124.0 63.4 %psum.85 = f32[16]{0:T(128)S(1)} all-reduce(f32[16]{0:T(128)S(1)} %get-tuple-element.63), channel_id=1, replica_groups=mesh['patch'=16,'col'=8] {'patch','col'}, use_global_device_ids=true, to_apply=%region_4.0 | all-reduce | flops 16 | bytes 128 | tf_op jit(solution)/shard_map/psum | solution.py:106
  187.6 63.0 %psum.86 = f32[16]{0:T(128)S(1)} all-reduce(f32[16]{0:T(128)S(1)} %multiply_reduce_fusion.9), channel_id=1, replica_groups=mesh['patch'=16,'col'=8] {'patch','col'}, use_global_device_ids=true, to_apply=%region_6.0 | all-reduce | flops 16 | bytes 128 | tf_op jit(solution)/shard_map/psum | solution.py:109
  252.1 4.0 collective-permute-start.5
  256.0 13.8 %all_gather.23 = f32[32,16,128]{2,1,0:T(8,128)S(1)} all-gather(f32[4,16,128]{2,1,0:T(8,128)S(1)} %fusion.44), channel_id=1, replica_groups=mesh['patch'=16,'col'=8] {'col'}, dimensions={0}, use_global_device_ids=true | all-gather | bytes 294912 | tf_op jit(solution)/shard_map/all_gather | solution.py:61
  270.5 7.5 multiply_reduce_fusion.8
  278.0 64.4 %psum.87 = f32[16]{0:T(128)S(1)} all-reduce(f32[16]{0:T(128)S(1)} %get-tuple-element.65), channel_id=1, replica_groups=mesh['patch'=16,'col'=8] {'patch','col'}, use_global_device_ids=true, to_apply=%region_8.0 | all-reduce | flops 16 | bytes 128 | tf_op jit(solution)/shard_map/psum | solution.py:106
  342.6 62.5 %psum.88 = f32[16]{0:T(128)S(1)} all-reduce(f32[16]{0:T(128)S(1)} %multiply_reduce_fusion.7), channel_id=1, replica_groups=mesh['patch'=16,'col'=8] {'patch','col'}, use_global_device_ids=true, to_apply=%region_10.0 | all-reduce | flops 16 | bytes 128 | tf_op jit(solution)/shard_map/psum | solution.py:106
  405.3 64.0 %psum.89 = f32[16]{0:T(128)S(1)} all-reduce(f32[16]{0:T(128)S(1)} %multiply_reduce_fusion.6), channel_id=1, replica_groups=mesh['patch'=16,'col'=8] {'patch','col'}, use_global_device_ids=true, to_apply=%region_12.0 | all-reduce | flops 16 | bytes 128 | tf_op jit(solution)/shard_map/psum | solution.py:109
  476.7 4.8 collective-permute-start.7
  481.5 14.5 %all_gather.24 = f32[32,16,128]{2,1,0:T(8,128)S(1)} all-gather(f32[4,16,128]{2,1,0:T(8,128)S(1)} %add_add_fusion.1), channel_id=1, replica_groups=mesh['patch'=16,'col'=8] {'col'}, dimensions={0}, use_global_device_ids=true | all-gather | bytes 294912 | tf_op jit(solution)/shard_map/all_gather | solution.py:61
  496.7 7.5 multiply_reduce_fusion.5
  504.2 61.8 %psum.90 = f32[16]{0:T(128)S(1)} all-reduce(f32[16]{0:T(128)S(1)} %get-tuple-element.67), channel_id=1, replica_groups=mesh['patch'=16,'col'=8] {'patch','col'}, use_global_device_ids=true, to_apply=%region_16.0 | all-reduce | flops 16 | bytes 128 | tf_op jit(solution)/shard_map/psum | solution.py:91
  571.4 13.9 %all_gather.25 = f32[32,16,128]{2,1,0:T(8,128)S(1)} all-gather(f32[4,16,128]{2,1,0:T(8,128)S(1)} %fusion.45), channel_id=1, replica_groups=mesh['patch'=16,'col'=8] {'col'}, dimensions={0}, use_global_device_ids=true | all-gather | bytes 294912 | tf_op jit(solution)/shard_map/all_gather | solution.py:61
  586.0 7.5 multiply_reduce_fusion.4
  593.5 63.5 %psum.91 = f32[16]{0:T(128)S(1)} all-reduce(f32[16]{0:T(128)S(1)} %get-tuple-element.69), channel_id=1, replica_groups=mesh['patch'=16,'col'=8] {'patch','col'}, use_global_device_ids=true, to_apply=%region_18.0 | all-reduce | flops 16 | bytes 128 | tf_op jit(solution)/shard_map/psum | solution.py:106
  657.1 62.6 %psum.92 = f32[16]{0:T(128)S(1)} all-reduce(f32[16]{0:T(128)S(1)} %multiply_reduce_fusion.3), channel_id=1, replica_groups=mesh['patch'=16,'col'=8] {'patch','col'}, use_global_device_ids=true, to_apply=%region_20.0 | all-reduce | flops 16 | bytes 128 | tf_op jit(solution)/shard_map/psum | solution.py:109
  721.1 4.0 collective-permute-start.11
  725.0 14.0 %all_gather.26 = f32[32,16,128]{2,1,0:T(8,128)S(1)} all-gather(f32[4,16,128]{2,1,0:T(8,128)S(1)} %fusion.46), channel_id=1, replica_groups=mesh['patch'=16,'col'=8] {'col'}, dimensions={0}, use_global_device_ids=true | all-gather | bytes 294912 | tf_op jit(solution)/shard_map/all_gather | solution.py:61
  739.8 7.5 multiply_reduce_fusion.2
  747.2 64.4 %psum.93 = f32[16]{0:T(128)S(1)} all-reduce(f32[16]{0:T(128)S(1)} %get-tuple-element.71), channel_id=1, replica_groups=mesh['patch'=16,'col'=8] {'patch','col'}, use_global_device_ids=true, to_apply=%region_22.0 | all-reduce | flops 16 | bytes 128 | tf_op jit(solution)/shard_map/psum | solution.py:106
  811.8 62.5 %psum.94 = f32[16]{0:T(128)S(1)} all-reduce(f32[16]{0:T(128)S(1)} %multiply_reduce_fusion.1), channel_id=1, replica_groups=mesh['patch'=16,'col'=8] {'patch','col'}, use_global_device_ids=true, to_apply=%region_24.0 | all-reduce | flops 16 | bytes 128 | tf_op jit(solution)/shard_map/psum | solution.py:106
  874.5 64.0 %psum.95 = f32[16]{0:T(128)S(1)} all-reduce(f32[16]{0:T(128)S(1)} %multiply_reduce_fusion), channel_id=1, replica_groups=mesh['patch'=16,'col'=8] {'patch','col'}, use_global_device_ids=true, to_apply=%region_26.0 | all-reduce | flops 16 | bytes 128 | tf_op jit(solution)/shard_map/psum | solution.py:109
  946.0 4.8 collective-permute-start.13
  950.8 14.3 %all_gather.27 = f32[32,16,128]{2,1,0:T(8,128)S(1)} all-gather(f32[4,16,128]{2,1,0:T(8,128)S(1)} %add_add_fusion), channel_id=1, replica_groups=mesh['patch'=16,'col'=8] {'col'}, dimensions={0}, use_global_device_ids=true | all-gather | bytes 294912 | tf_op jit(solution)/shard_map/all_gather | solution.py:61
  965.8 8.0 fusion.3
  (115 shorter events, 34.3 us)
Async XLA Ops:
  0.6 95.9 %copy-start = (f32[4,128,128]{2,1,0:T(8,128)S(1)}, f32[4,128,128]{2,1,0:T(8,128)}, u32[]{:S(2)}) copy-start(f32[4,128,128]{2,1,0:T(8,128)} %param.28) | copy-start | bytes 786436
  0.6 115.9 %copy-start.1 = (f32[4,16,128]{2,1,0:T(8,128)S(1)}, f32[4,16,128]{2,1,0:T(8,128)}, u32[]{:S(2)}) copy-start(f32[4,16,128]{2,1,0:T(8,128)} %param.24) | copy-start | bytes 98308
  0.7 115.9 %copy-start.6 = (f32[4,128]{1,0:T(4,128)S(1)}, f32[4,128]{1,0:T(4,128)}, u32[]{:S(2)}) copy-start(f32[4,128]{1,0:T(4,128)} %param.26) | copy-start | bytes 6148
  0.7 115.9 %copy-start.5 = (f32[4,128]{1,0:T(4,128)S(1)}, f32[4,128]{1,0:T(4,128)}, u32[]{:S(2)}) copy-start(f32[4,128]{1,0:T(4,128)} %param.29) | copy-start | bytes 6148
  0.7 115.9 %copy-start.4 = (f32[4,128]{1,0:T(4,128)S(1)}, f32[4,128]{1,0:T(4,128)}, u32[]{:S(2)}) copy-start(f32[4,128]{1,0:T(4,128)} %param.30) | copy-start | bytes 6148
  0.7 23.3 %collective-permute-start = (f32[4,16,128]{2,1,0:T(8,128)}, f32[4,16,128]{2,1,0:T(8,128)S(1)}, u32[]{:S(2)}, u32[]{:S(2)}) collective-permute-start(f32[4,16,128]{2,1,0:T(8,128)} %param.24), channel_id=1, source_target_pairs={{0,8},{8,16},{16,24},{24,32},{32,40},{40,48},{48,56},{56,64},{64,7... | collective-permute-start | bytes 98312 | tf_op jit(solution)/shard_map/ppermute | solution.py:15
  2.8 21.2 %collective-permute-start.1 = (f32[4,16,128]{2,1,0:T(8,128)}, f32[4,16,128]{2,1,0:T(8,128)S(1)}, u32[]{:S(2)}, u32[]{:S(2)}) collective-permute-start(f32[4,16,128]{2,1,0:T(8,128)} %param.24), channel_id=1, source_target_pairs={{0,120},{8,0},{16,8},{24,16},{32,24},{40,32},{48,40},{56,48},{64,5... | collective-permute-start | bytes 98312 | tf_op jit(solution)/shard_map/ppermute | solution.py:15
  97.1 18.7 %collective-permute-start.2 = (f32[4,16,128]{2,1,0:T(8,128)S(1)}, f32[4,16,128]{2,1,0:T(8,128)S(1)}, u32[]{:S(2)}, u32[]{:S(2)}) collective-permute-start(f32[4,16,128]{2,1,0:T(8,128)S(1)} %fusion.43), channel_id=1, source_target_pairs={{0,8},{8,16},{16,24},{24,32},{32,40},{40,48},{48,56},{56,64},{64,7... | collective-permute-start | bytes 98312 | tf_op jit(solution)/shard_map/ppermute | solution.py:15
  97.3 18.4 %collective-permute-start.3 = (f32[4,16,128]{2,1,0:T(8,128)S(1)}, f32[4,16,128]{2,1,0:T(8,128)S(1)}, u32[]{:S(2)}, u32[]{:S(2)}) collective-permute-start(f32[4,16,128]{2,1,0:T(8,128)S(1)} %fusion.43), channel_id=1, source_target_pairs={{0,120},{8,0},{16,8},{24,16},{32,24},{40,32},{48,40},{56,48},{64,5... | collective-permute-start | bytes 98312 | tf_op jit(solution)/shard_map/ppermute | solution.py:15
  251.2 18.6 %collective-permute-start.4 = (f32[4,16,128]{2,1,0:T(8,128)S(1)}, f32[4,16,128]{2,1,0:T(8,128)S(1)}, u32[]{:S(2)}, u32[]{:S(2)}) collective-permute-start(f32[4,16,128]{2,1,0:T(8,128)S(1)} %fusion.44), channel_id=1, source_target_pairs={{0,8},{8,16},{16,24},{24,32},{32,40},{40,48},{48,56},{56,64},{64,7... | collective-permute-start | bytes 98312 | tf_op jit(solution)/shard_map/ppermute | solution.py:15
  252.1 17.7 %collective-permute-start.5 = (f32[4,16,128]{2,1,0:T(8,128)S(1)}, f32[4,16,128]{2,1,0:T(8,128)S(1)}, u32[]{:S(2)}, u32[]{:S(2)}) collective-permute-start(f32[4,16,128]{2,1,0:T(8,128)S(1)} %fusion.44), channel_id=1, source_target_pairs={{0,120},{8,0},{16,8},{24,16},{32,24},{40,32},{48,40},{56,48},{64,5... | collective-permute-start | bytes 98312 | tf_op jit(solution)/shard_map/ppermute | solution.py:15
  269.8 226.9 %copy-start.2 = (f32[4,16,128]{2,1,0:T(8,128)S(1)}, f32[4,16,128]{2,1,0:T(8,128)}, u32[]{:S(2)}) copy-start(f32[4,16,128]{2,1,0:T(8,128)} %param.25) | copy-start | bytes 98308
  476.7 19.3 %collective-permute-start.6 = (f32[4,16,128]{2,1,0:T(8,128)S(1)}, f32[4,16,128]{2,1,0:T(8,128)S(1)}, u32[]{:S(2)}, u32[]{:S(2)}) collective-permute-start(f32[4,16,128]{2,1,0:T(8,128)S(1)} %add_add_fusion.1), channel_id=1, source_target_pairs={{0,8},{8,16},{16,24},{24,32},{32,40},{40,48},{48,56},{56,64},{64,7... | collective-permute-start | bytes 98312 | tf_op jit(solution)/shard_map/ppermute | solution.py:15
  476.7 19.3 %collective-permute-start.7 = (f32[4,16,128]{2,1,0:T(8,128)S(1)}, f32[4,16,128]{2,1,0:T(8,128)S(1)}, u32[]{:S(2)}, u32[]{:S(2)}) collective-permute-start(f32[4,16,128]{2,1,0:T(8,128)S(1)} %add_add_fusion.1), channel_id=1, source_target_pairs={{0,120},{8,0},{16,8},{24,16},{32,24},{40,32},{48,40},{56,48},{64,5... | collective-permute-start | bytes 98312 | tf_op jit(solution)/shard_map/ppermute | solution.py:15
  566.6 18.7 %collective-permute-start.8 = (f32[4,16,128]{2,1,0:T(8,128)S(1)}, f32[4,16,128]{2,1,0:T(8,128)S(1)}, u32[]{:S(2)}, u32[]{:S(2)}) collective-permute-start(f32[4,16,128]{2,1,0:T(8,128)S(1)} %fusion.45), channel_id=1, source_target_pairs={{0,8},{8,16},{16,24},{24,32},{32,40},{40,48},{48,56},{56,64},{64,7... | collective-permute-start | bytes 98312 | tf_op jit(solution)/shard_map/ppermute | solution.py:15
  567.7 17.5 %collective-permute-start.9 = (f32[4,16,128]{2,1,0:T(8,128)S(1)}, f32[4,16,128]{2,1,0:T(8,128)S(1)}, u32[]{:S(2)}, u32[]{:S(2)}) collective-permute-start(f32[4,16,128]{2,1,0:T(8,128)S(1)} %fusion.45), channel_id=1, source_target_pairs={{0,120},{8,0},{16,8},{24,16},{32,24},{40,32},{48,40},{56,48},{64,5... | collective-permute-start | bytes 98312 | tf_op jit(solution)/shard_map/ppermute | solution.py:15
  720.2 18.8 %collective-permute-start.10 = (f32[4,16,128]{2,1,0:T(8,128)S(1)}, f32[4,16,128]{2,1,0:T(8,128)S(1)}, u32[]{:S(2)}, u32[]{:S(2)}) collective-permute-start(f32[4,16,128]{2,1,0:T(8,128)S(1)} %fusion.46), channel_id=1, source_target_pairs={{0,8},{8,16},{16,24},{24,32},{32,40},{40,48},{48,56},{56,64},{64,7... | collective-permute-start | bytes 98312 | tf_op jit(solution)/shard_map/ppermute | solution.py:15
  721.1 17.9 %collective-permute-start.11 = (f32[4,16,128]{2,1,0:T(8,128)S(1)}, f32[4,16,128]{2,1,0:T(8,128)S(1)}, u32[]{:S(2)}, u32[]{:S(2)}) collective-permute-start(f32[4,16,128]{2,1,0:T(8,128)S(1)} %fusion.46), channel_id=1, source_target_pairs={{0,120},{8,0},{16,8},{24,16},{32,24},{40,32},{48,40},{56,48},{64,5... | collective-permute-start | bytes 98312 | tf_op jit(solution)/shard_map/ppermute | solution.py:15
  945.9 27.9 %copy-start.3 = (f32[4,16,128]{2,1,0:T(8,128)}, f32[4,16,128]{2,1,0:T(8,128)S(1)}, u32[]{:S(2)}) copy-start(f32[4,16,128]{2,1,0:T(8,128)S(1)} %add_add_fusion) | copy-start | bytes 98308
  945.9 19.2 %collective-permute-start.12 = (f32[4,16,128]{2,1,0:T(8,128)S(1)}, f32[4,16,128]{2,1,0:T(8,128)S(1)}, u32[]{:S(2)}, u32[]{:S(2)}) collective-permute-start(f32[4,16,128]{2,1,0:T(8,128)S(1)} %add_add_fusion), channel_id=1, source_target_pairs={{0,8},{8,16},{16,24},{24,32},{32,40},{40,48},{48,56},{56,64},{64,7... | collective-permute-start | bytes 98312 | tf_op jit(solution)/shard_map/ppermute | solution.py:15
  946.0 19.1 %collective-permute-start.13 = (f32[4,16,128]{2,1,0:T(8,128)S(1)}, f32[4,16,128]{2,1,0:T(8,128)S(1)}, u32[]{:S(2)}, u32[]{:S(2)}) collective-permute-start(f32[4,16,128]{2,1,0:T(8,128)S(1)} %add_add_fusion), channel_id=1, source_target_pairs={{0,120},{8,0},{16,8},{24,16},{32,24},{40,32},{48,40},{56,48},{64,5... | collective-permute-start | bytes 98312 | tf_op jit(solution)/shard_map/ppermute | solution.py:15
where the time goes:
time: 984 us; the launch traced here: 974 us
  blocking collectives  860 us (87%)
  matrix products  55.7 us (6%)
  starting transfers between devices  34.8 us (4%)
  other arithmetic  16.5 us (2%)
    psum x6, blocking collectives, body(): coeff = lax.psum(column_sum(basis[place], image), ('patch', 'col'))  381 us
    psum x4, blocking collectives, body(): norm = jnp.sqrt(lax.psum(column_sum(image, image), ('patch', 'col')) + EPS)  254 us
    psum x2, blocking collectives, body(): beta = jnp.sqrt(lax.psum(column_sum(start, start), ('patch', 'col')) + EPS)  126 us
    all_gather x7, blocking collectives, near_field(): own_patch = lax.all_gather(field, 'col', axis=0, tiled=True)  99.4 us
    dot_general x7, matrix products, near_field(): jnp.einsum('bkij,bkcj->bci', nearfield, sources * live_mask[:, :, None, N...  52.9 us
    ppermute x14, starting transfers between devices, from_behind(): lax.ppermute(array, axis, [(i, (i + by) % size) for i in range(size)])  34.8 us
  transfers between devices with their start and end apart: 14, of which 0 were waited for; matrix products, arithmetic and copies ran while one was open for 0% of the time, Pallas kernels for 0%

commit v1 on v0

--- a/solution.py
+++ b/solution.py
@@ -58,7 +58,9 @@
     conduct = conductance[:, None, :]
 
     def near_field(field):
-        own_patch = lax.all_gather(field, "col", axis=0, tiled=True)
+        own_patch = jnp.concatenate(
+            lax.all_to_all(jnp.stack([field] * lax.axis_size("col")), "col", 0, 0), axis=0
+        )
         before = from_behind(field, "patch", 1)
         following = from_behind(field, "patch", -1)
         stacked = jnp.concatenate([own_patch, before, following], axis=0)

time: 984 us -> 952 us (0.967)
  blocking collectives: 860 us -> 774 us
  starting transfers between devices: 34.8 us -> 66.4 us
  waiting for transfers between devices: 0.04 us -> 15.7 us
    all_gather x7 -> x0, blocking collectives: 99.4 us -> none  [near_field(): own_patch = lax.all_gather(field, 'col', axis=0, tiled=True)]
    all_to_all x0 -> x7, starting transfers between devices: none -> 31.2 us  [near_field(): lax.all_to_all(jnp.stack([field] * lax.axis_size('col')), 'col', 0, 0)]
    psum x6, blocking collectives: 381 us -> 391 us  [body(): coeff = lax.psum(column_sum(basis[place], image), ('patch', 'col'))]
  transfers between devices with their start and end apart: 14 -> 21, of which waited for: 0 -> 14; matrix products, arithmetic and copies ran while one was open for 0% -> 0% of each run, Pallas kernels for 0% -> 0%
where the time goes in v1:
time: 952 us; the launch traced here: 941 us
  blocking collectives  774 us (81%)
  starting transfers between devices  66.4 us (7%)
  matrix products  55.7 us (6%)
  other arithmetic  16.5 us (2%)
  waiting for transfers between devices  15.7 us (2%)
  local copies, waits for them, and re-layouts  12 us (1%)
    psum x6, blocking collectives, body(): coeff = lax.psum(column_sum(basis[place], image), ('patch', 'col'))  391 us
    psum x4, blocking collectives, body(): norm = jnp.sqrt(lax.psum(column_sum(image, image), ('patch', 'col')) + EPS)  253 us
    psum x2, blocking collectives, body(): beta = jnp.sqrt(lax.psum(column_sum(start, start), ('patch', 'col')) + EPS)  130 us
    dot_general x7, matrix products, near_field(): jnp.einsum('bkij,bkcj->bci', nearfield, sources * live_mask[:, :, None, N...  52.9 us
    ppermute x14, starting transfers between devices, from_behind(): lax.ppermute(array, axis, [(i, (i + by) % size) for i in range(size)])  35.3 us
    all_to_all x7, starting transfers between devices, near_field(): lax.all_to_all(jnp.stack([field] * lax.axis_size('col')), 'col', 0, 0)  31.2 us
  transfers between devices with their start and end apart: 21, of which 14 were waited for; matrix products, arithmetic and copies ran while one was open for 0% of the time, Pallas kernels for 0%

profile of v1, /device:TPU:1, one launch (start us, length us, event | category | flops | bytes accessed | tf_op | source)
XLA Modules:
  0.0 941.2 jit_solution(12412474038883919479)
XLA Ops:
  8.1 6.3 all-to-all-start
  16.7 4.2 all-to-all-done
  21.6 7.6 multiply_reduce_fusion.11
  29.2 63.6 %psum.84 = f32[16]{0:T(128)S(1)} all-reduce(f32[16]{0:T(128)S(1)} %get-tuple-element.61), channel_id=1, replica_groups=mesh['patch'=16,'col'=8] {'patch','col'}, use_global_device_ids=true, to_apply=%region_2.0 | all-reduce | flops 16 | bytes 128 | tf_op jit(solution)/shard_map/psum | solution.py:93
  94.1 4.2 all-to-all-start.1
  98.3 4.8 collective-permute-start.3
  105.9 7.5 multiply_reduce_fusion.10
  113.4 66.1 %psum.85 = f32[16]{0:T(128)S(1)} all-reduce(f32[16]{0:T(128)S(1)} %get-tuple-element.63), channel_id=1, replica_groups=mesh['patch'=16,'col'=8] {'patch','col'}, use_global_device_ids=true, to_apply=%region_4.0 | all-reduce | flops 16 | bytes 128 | tf_op jit(solution)/shard_map/psum | solution.py:108
  179.7 63.2 %psum.86 = f32[16]{0:T(128)S(1)} all-reduce(f32[16]{0:T(128)S(1)} %multiply_reduce_fusion.9), channel_id=1, replica_groups=mesh['patch'=16,'col'=8] {'patch','col'}, use_global_device_ids=true, to_apply=%region_6.0 | all-reduce | flops 16 | bytes 128 | tf_op jit(solution)/shard_map/psum | solution.py:111
  244.1 4.2 all-to-all-start.2
  248.5 5.2 collective-permute-start.5
  255.9 7.5 multiply_reduce_fusion.8
  263.4 66.6 %psum.87 = f32[16]{0:T(128)S(1)} all-reduce(f32[16]{0:T(128)S(1)} %get-tuple-element.65), channel_id=1, replica_groups=mesh['patch'=16,'col'=8] {'patch','col'}, use_global_device_ids=true, to_apply=%region_8.0 | all-reduce | flops 16 | bytes 128 | tf_op jit(solution)/shard_map/psum | solution.py:108
  330.2 63.2 %psum.88 = f32[16]{0:T(128)S(1)} all-reduce(f32[16]{0:T(128)S(1)} %multiply_reduce_fusion.7), channel_id=1, replica_groups=mesh['patch'=16,'col'=8] {'patch','col'}, use_global_device_ids=true, to_apply=%region_10.0 | all-reduce | flops 16 | bytes 128 | tf_op jit(solution)/shard_map/psum | solution.py:108
  393.6 63.0 %psum.89 = f32[16]{0:T(128)S(1)} all-reduce(f32[16]{0:T(128)S(1)} %multiply_reduce_fusion.6), channel_id=1, replica_groups=mesh['patch'=16,'col'=8] {'patch','col'}, use_global_device_ids=true, to_apply=%region_12.0 | all-reduce | flops 16 | bytes 128 | tf_op jit(solution)/shard_map/psum | solution.py:111
  464.7 4.0 all-to-all-start.3
  469.3 4.2 collective-permute-start.7
  476.2 7.5 multiply_reduce_fusion.5
  483.7 66.1 %psum.90 = f32[16]{0:T(128)S(1)} all-reduce(f32[16]{0:T(128)S(1)} %get-tuple-element.67), channel_id=1, replica_groups=mesh['patch'=16,'col'=8] {'patch','col'}, use_global_device_ids=true, to_apply=%region_16.0 | all-reduce | flops 16 | bytes 128 | tf_op jit(solution)/shard_map/psum | solution.py:93
  551.1 4.2 all-to-all-start.4
  555.5 4.8 collective-permute-start.9
  562.9 7.5 multiply_reduce_fusion.4
  570.3 66.3 %psum.91 = f32[16]{0:T(128)S(1)} all-reduce(f32[16]{0:T(128)S(1)} %get-tuple-element.69), channel_id=1, replica_groups=mesh['patch'=16,'col'=8] {'patch','col'}, use_global_device_ids=true, to_apply=%region_18.0 | all-reduce | flops 16 | bytes 128 | tf_op jit(solution)/shard_map/psum | solution.py:108
  636.8 63.2 %psum.92 = f32[16]{0:T(128)S(1)} all-reduce(f32[16]{0:T(128)S(1)} %multiply_reduce_fusion.3), channel_id=1, replica_groups=mesh['patch'=16,'col'=8] {'patch','col'}, use_global_device_ids=true, to_apply=%region_20.0 | all-reduce | flops 16 | bytes 128 | tf_op jit(solution)/shard_map/psum | solution.py:111
  701.3 4.2 all-to-all-start.5
  705.5 4.8 collective-permute-start.11
  713.0 7.5 multiply_reduce_fusion.2
  720.5 66.1 %psum.93 = f32[16]{0:T(128)S(1)} all-reduce(f32[16]{0:T(128)S(1)} %get-tuple-element.71), channel_id=1, replica_groups=mesh['patch'=16,'col'=8] {'patch','col'}, use_global_device_ids=true, to_apply=%region_22.0 | all-reduce | flops 16 | bytes 128 | tf_op jit(solution)/shard_map/psum | solution.py:108
  786.8 63.2 %psum.94 = f32[16]{0:T(128)S(1)} all-reduce(f32[16]{0:T(128)S(1)} %multiply_reduce_fusion.1), channel_id=1, replica_groups=mesh['patch'=16,'col'=8] {'patch','col'}, use_global_device_ids=true, to_apply=%region_24.0 | all-reduce | flops 16 | bytes 128 | tf_op jit(solution)/shard_map/psum | solution.py:108
  850.2 63.3 %psum.95 = f32[16]{0:T(128)S(1)} all-reduce(f32[16]{0:T(128)S(1)} %multiply_reduce_fusion), channel_id=1, replica_groups=mesh['patch'=16,'col'=8] {'patch','col'}, use_global_device_ids=true, to_apply=%region_26.0 | all-reduce | flops 16 | bytes 128 | tf_op jit(solution)/shard_map/psum | solution.py:111
  926.0 4.2 collective-permute-start.13
  933.0 8.0 fusion.3
  (129 shorter events, 53.9 us)
Async XLA Ops:
  0.6 92.2 %copy-start = (f32[4,128,128]{2,1,0:T(8,128)S(1)}, f32[4,128,128]{2,1,0:T(8,128)}, u32[]{:S(2)}) copy-start(f32[4,128,128]{2,1,0:T(8,128)} %param.28) | copy-start | bytes 786436
  0.6 16.0 %collective-permute-start = (f32[4,16,128]{2,1,0:T(8,128)}, f32[4,16,128]{2,1,0:T(8,128)S(1)}, u32[]{:S(2)}, u32[]{:S(2)}) collective-permute-start(f32[4,16,128]{2,1,0:T(8,128)} %param.24), channel_id=1, source_target_pairs={{0,8},{8,16},{16,24},{24,32},{32,40},{40,48},{48,56},{56,64},{64,7... | collective-permute-start | bytes 98312 | tf_op jit(solution)/shard_map/ppermute | solution.py:15
  2.8 13.9 %collective-permute-start.1 = (f32[4,16,128]{2,1,0:T(8,128)}, f32[4,16,128]{2,1,0:T(8,128)S(1)}, u32[]{:S(2)}, u32[]{:S(2)}) collective-permute-start(f32[4,16,128]{2,1,0:T(8,128)} %param.24), channel_id=1, source_target_pairs={{0,120},{8,0},{16,8},{24,16},{32,24},{40,32},{48,40},{56,48},{64,5... | collective-permute-start | bytes 98312 | tf_op jit(solution)/shard_map/ppermute | solution.py:15
  8.1 12.8 %all-to-all-start = ((f32[8,4,16,128]{3,2,1,0:T(8,128)}), f32[8,4,16,128]{3,2,1,0:T(8,128)S(1)}, u32[]{:S(2)}, u32[]{:S(2)}) async-start(f32[8,4,16,128]{3,2,1,0:T(8,128)} %stack.42), calls=%async_computation | async-start | bytes 524288 | tf_op jit(solution)/shard_map/all_to_all | solution.py:62
  20.9 85.0 %copy-start.1 = (f32[4,16,128]{2,1,0:T(8,128)S(1)}, f32[4,16,128]{2,1,0:T(8,128)}, u32[]{:S(2)}) copy-start(f32[4,16,128]{2,1,0:T(8,128)} %param.24) | copy-start | bytes 98308
  20.9 85.0 %copy-start.4 = (f32[4,128]{1,0:T(4,128)S(1)}, f32[4,128]{1,0:T(4,128)}, u32[]{:S(2)}) copy-start(f32[4,128]{1,0:T(4,128)} %param.30) | copy-start | bytes 6148
  20.9 85.0 %copy-start.5 = (f32[4,128]{1,0:T(4,128)S(1)}, f32[4,128]{1,0:T(4,128)}, u32[]{:S(2)}) copy-start(f32[4,128]{1,0:T(4,128)} %param.29) | copy-start | bytes 6148
  20.9 85.0 %copy-start.6 = (f32[4,128]{1,0:T(4,128)S(1)}, f32[4,128]{1,0:T(4,128)}, u32[]{:S(2)}) copy-start(f32[4,128]{1,0:T(4,128)} %param.26) | copy-start | bytes 6148
  94.1 11.1 %all-to-all-start.1 = ((f32[8,4,16,128]{3,2,1,0:T(8,128)}), f32[8,4,16,128]{3,2,1,0:T(8,128)S(1)}, u32[]{:S(2)}, u32[]{:S(2)}) async-start(f32[8,4,16,128]{3,2,1,0:T(8,128)} %stack.43), calls=%async_computation.1 | async-start | bytes 524288 | tf_op jit(solution)/shard_map/all_to_all | solution.py:62
  98.3 6.1 collective-permute-start.2
  98.3 6.1 collective-permute-start.3
  244.1 11.1 %all-to-all-start.2 = ((f32[8,4,16,128]{3,2,1,0:T(8,128)}), f32[8,4,16,128]{3,2,1,0:T(8,128)S(1)}, u32[]{:S(2)}, u32[]{:S(2)}) async-start(f32[8,4,16,128]{3,2,1,0:T(8,128)} %stack.47), calls=%async_computation.2 | async-start | bytes 524288 | tf_op jit(solution)/shard_map/all_to_all | solution.py:62
  248.4 6.1 collective-permute-start.4
  248.5 6.2 collective-permute-start.5
  255.2 221.0 %copy-start.2 = (f32[4,16,128]{2,1,0:T(8,128)S(1)}, f32[4,16,128]{2,1,0:T(8,128)}, u32[]{:S(2)}) copy-start(f32[4,16,128]{2,1,0:T(8,128)} %param.25) | copy-start | bytes 98308
  464.7 10.8 %all-to-all-start.3 = ((f32[8,4,16,128]{3,2,1,0:T(8,128)}), f32[8,4,16,128]{3,2,1,0:T(8,128)S(1)}, u32[]{:S(2)}, u32[]{:S(2)}) async-start(f32[8,4,16,128]{3,2,1,0:T(8,128)} %stack.52), calls=%async_computation.3 | async-start | bytes 524288 | tf_op jit(solution)/shard_map/all_to_all | solution.py:62
  468.7 6.1 collective-permute-start.6
  469.3 5.5 collective-permute-start.7
  551.1 11.0 %all-to-all-start.4 = ((f32[8,4,16,128]{3,2,1,0:T(8,128)}), f32[8,4,16,128]{3,2,1,0:T(8,128)S(1)}, u32[]{:S(2)}, u32[]{:S(2)}) async-start(f32[8,4,16,128]{3,2,1,0:T(8,128)} %stack.53), calls=%async_computation.4 | async-start | bytes 524288 | tf_op jit(solution)/shard_map/all_to_all | solution.py:62
  555.3 6.2 collective-permute-start.8
  555.5 6.1 collective-permute-start.9
  701.3 11.1 %all-to-all-start.5 = ((f32[8,4,16,128]{3,2,1,0:T(8,128)}), f32[8,4,16,128]{3,2,1,0:T(8,128)S(1)}, u32[]{:S(2)}, u32[]{:S(2)}) async-start(f32[8,4,16,128]{3,2,1,0:T(8,128)} %stack.57), calls=%async_computation.5 | async-start | bytes 524288 | tf_op jit(solution)/shard_map/all_to_all | solution.py:62
  705.5 6.1 collective-permute-start.10
  705.5 6.1 collective-permute-start.11
  920.8 20.2 %copy-start.3 = (f32[4,16,128]{2,1,0:T(8,128)}, f32[4,16,128]{2,1,0:T(8,128)S(1)}, u32[]{:S(2)}) copy-start(f32[4,16,128]{2,1,0:T(8,128)S(1)} %add_add_fusion) | copy-start | bytes 98308
  921.5 10.8 %all-to-all-start.6 = ((f32[8,4,16,128]{3,2,1,0:T(8,128)}), f32[8,4,16,128]{3,2,1,0:T(8,128)S(1)}, u32[]{:S(2)}, u32[]{:S(2)}) async-start(f32[8,4,16,128]{3,2,1,0:T(8,128)} %stack.62), calls=%async_computation.6 | async-start | bytes 524288 | tf_op jit(solution)/shard_map/all_to_all | solution.py:62
  925.4 6.1 collective-permute-start.12
  926.0 5.5 collective-permute-start.13
